TPU v7x, 32 devices: a whole 2x2x4 slice. The times are simulated.
32 devices in a mesh: pts: 8 (over y, x, core), val: 4 (over z).
Axes of the slice: x: 2, y: 2, z: 4, core: 2. Of those that a mesh axis runs over, the one named last changes fastest.
Arguments:
- trials: bfloat16 [2, 1024, 1024], P(None, 'val', 'pts'), may hold values from -6 to 6
- psi_val: bfloat16 [8192, 1024], P('pts', 'val'), may hold values from -0.1875 to 0.1875
- psi_cond: bfloat16 [8192, 1024], P('pts'), may hold values from -0.1875 to 0.1875
- kernel: bfloat16 [8192, 8192], P(None, ('pts', 'val')), may hold values from -0.5 to 0.5
- eps_val: float32 [1024], P('val'), may hold values from -1.75 to -0.25
- eps_cond: float32 [1024], replicated, may hold values from 0.5 to 1.5
Outputs:
- first: float32 [2, 1024, 1024], P(None, 'val', 'pts')
- filtered: float32 [2, 1024, 1024], P(None, 'val', 'pts')
All inputs are finite; a program needn't handle non-finite values.
Results may differ from a plain program's by a relative error of at most 0.025.
Values may be sent and summed in bfloat16 or wider, within the bound.
A program may use at most 64 MiB of HBM per device.

v0:
```python
import jax
import jax.numpy as jnp
from jax import lax
from jax.sharding import PartitionSpec as P

center_shift = 1.75
half_width = 1.25


def gathered_inner(local_trial, psi_cond):
    return jnp.einsum(
        "kvc,mc->kvm",
        lax.all_gather(local_trial, "pts", axis=2, tiled=True),
        psi_cond,
        preferred_element_type=jnp.float32,
    )


def orbital_terms(inner, psi_val, psi_cond, kernel):
    rho_part = jnp.einsum("mv,kvm->km", psi_val.astype(jnp.float32), inner)
    rho = lax.psum_scatter(rho_part, "val", scatter_dimension=1, tiled=True).astype(jnp.bfloat16)
    image_part = jnp.einsum("km,nm->kn", rho, kernel, preferred_element_type=jnp.float32)
    image_rows = lax.psum_scatter(
        image_part.astype(jnp.bfloat16), "pts", scatter_dimension=1, tiled=True
    ).astype(jnp.float32)
    image = lax.psum(image_rows, "val")
    weighted = (jnp.transpose(psi_val.astype(jnp.float32))[None] * image[:, None, :]).astype(
        jnp.bfloat16
    )
    return jnp.einsum("kvm,mc->kvc", weighted, psi_cond, preferred_element_type=jnp.float32)


def reduced(partial_sum):
    return lax.psum_scatter(
        partial_sum.astype(jnp.bfloat16), "pts", scatter_dimension=2, tiled=True
    ).astype(jnp.float32)


def local(trials, psi_val, psi_cond, kernel, eps_val, eps_cond):
    cols_own = trials.shape[2]
    index_pts = lax.axis_index("pts")
    diff_whole = (eps_cond[None, :] - eps_val[:, None] - center_shift)[None]
    diff_own = lax.dynamic_slice_in_dim(diff_whole, index_pts * cols_own, cols_own, 2)
    first_image = reduced(
        orbital_terms(gathered_inner(trials, psi_cond), psi_val, psi_cond, kernel)
    )
    first = (diff_own * trials.astype(jnp.float32) + 2.0 * first_image) / half_width
    second_trial = first.astype(jnp.bfloat16)
    second_inner = gathered_inner(second_trial, psi_cond)
    second_image = reduced(orbital_terms(second_inner, psi_val, psi_cond, kernel))
    filtered = 2.0 * (
        diff_own * second_trial.astype(jnp.float32) + 2.0 * second_image
    ) / half_width - trials.astype(jnp.float32)
    return (first, filtered)


def solution(mesh):
    in_specs = (
        P(None, "val", "pts"),
        P("pts", "val"),
        P("pts", None),
        P(None, ("pts", "val")),
        P("val"),
        P(),
    )
    out_specs = (P(None, "val", "pts"), P(None, "val", "pts"))
    return jax.shard_map(local, mesh=mesh, in_specs=in_specs, out_specs=out_specs, check_vma=False)
```

profile of v0, /device:TPU:0, one launch (start us, length us, event | category | flops | bytes accessed | tf_op | source)
XLA Modules:
  0.0 326.2 jit_solution(14909899464436743166)
XLA Ops:
  7.2 0.0 copy-start
  7.2 0.0 all-gather.3.cloned.1.call-start
  7.2 0.7 all-gather.3.cloned.1.call-update
  7.9 0.0 reduce-scatter.15.cloned.1.call-start
  8.0 28.1 %all-gather.3.cloned.1.call-done = bf16[2,256,1024]{2,1,0:T(8,128)(2,1)} async-done(((bf16[2,256,128]{2,1,0:T(8,128)(2,1)}), bf16[2,256,1024]{2,1,0:T(8,128)(2,1)}) %all-gather.3.cloned.1.call-update) | async-done | bytes 1048592 | tf_op jit(solution)/shard_map/all_gather | solution.py:13
  36.1 0.0 copy-done
  36.1 2.5 fusion.6
  38.6 2.0 copy.10
  40.6 3.4 %fusion.20 = f32[1024,1,2]{2,1,0:T(1,128)} fusion(bf16[2,256,1024]{1,0,2:T(2,128)(2,1)} %copy.10, bf16[1024,256,1]{1,0,2:T(8,128)(2,1)} %bitcast.48), kind=kOutput, calls=%fused_computation.21 | convolution fusion | flops 1048576 | bytes 1581056 | tf_op jit(solution)/shard_map/mv,kvm->km/dot_general | solution.py:20
  44.0 0.0 reduce-scatter.15.cloned.1.call-update
  44.1 0.0 reduce-scatter.19.cloned.1.call-start
  44.1 22.0 %reduce-scatter.15.cloned.1.call-done = f32[2,256]{0,1:T(8,128)} async-done(((f32[2,1024]{0,1:T(8,128)}), f32[2,256]{0,1:T(8,128)}) %reduce-scatter.15.cloned.1.call-update) | async-done | bytes 2064 | tf_op jit(solution)/shard_map/reduce_scatter | solution.py:21
  66.1 3.4 %convolution_convert_fusion.1 = bf16[2,8192]{1,0:T(2,128)(2,1)S(1)} fusion(bf16[8192,256]{1,0:T(8,128)(2,1)} %param.9, f32[2,256]{0,1:T(8,128)} %reduce-scatter.15.cloned.1.call-done), kind=kOutput, calls=%fused_computation.1 | convolution fusion | flops 8405504 | bytes 4229120 | tf_op jit(solution)/shard_map/km,nm->kn/dot_general | solution.py:22
  69.5 1.9 copy.15
  71.4 0.0 reduce-scatter.19.cloned.1.call-update
  71.4 0.0 reduce-scatter.21.cloned.1.call-start
  71.5 1.1 convert_bitcast_fusion
  72.6 1.3 copy.9
  74.0 37.0 %reduce-scatter.19.cloned.1.call-done = bf16[1024,2]{1,0:T(8,128)(2,1)} async-done(((bf16[8192,2]{1,0:T(8,128)(2,1)}), bf16[1024,2]{1,0:T(8,128)(2,1)}) %reduce-scatter.19.cloned.1.call-update) | async-done | bytes 4112
  111.0 1.1 copy.16
  112.0 11.9 %psum.14 = f32[2,1024]{1,0:T(2,128)S(1)} all-reduce(bf16[2,1024]{1,0:T(2,128)(2,1)S(1)} %copy.16), channel_id=1, replica_groups=mesh['pts'=8,'val'=4] {'val'}, use_global_device_ids=true, to_apply=%region_2.0 | all-reduce | flops 2048 | bytes 12288 | tf_op jit(solution)/shard_map/psum | solution.py:26
  124.0 3.4 %fusion.8 = bf16[2,256,1024]{2,1,0:T(8,128)(2,1)} fusion(bf16[1024,1024]{1,0:T(8,128)(2,1)S(1)} %copy-done, f32[2,1024]{1,0:T(2,128)S(1)} %psum.14, f32[256,1024]{1,0:T(8,128)} %copy.9), kind=kOutput, calls=%fused_computation.12 | convolution fusion | flops 1075314688 | bytes 4202496 | tf_op jit(solution)/shard_map/kvm,mc->kvc/dot_general | solution.py:30
  127.4 2.5 copy.17
  129.9 0.0 copy-start.4
  129.9 0.0 copy-start.1
  130.0 1.2 copy.23
  131.2 0.0 reduce-scatter.21.cloned.1.call-update
  131.2 0.0 all-gather.5.cloned.1.call-start
  131.2 0.8 dynamic-slice.4
  132.0 0.0 copy-done.4
  132.0 0.1 subtract_add_fusion
  132.1 32.4 %reduce-scatter.21.cloned.1.call-done = bf16[128,512]{1,0:T(8,128)(2,1)} async-done(((bf16[1024,512]{1,0:T(8,128)(2,1)}), bf16[128,512]{1,0:T(8,128)(2,1)}) %reduce-scatter.21.cloned.1.call-update) | async-done | bytes 131088
  164.5 0.9 reshape.18
  165.5 0.1 copy.18
  165.6 0.0 copy-done.1
  165.6 0.8 fusion.26
  166.4 0.0 all-gather.5.cloned.1.call-update
  166.4 0.0 reduce-scatter.17.cloned.1.call-start
  166.5 23.8 %all-gather.5.cloned.1.call-done = bf16[2,256,1024]{2,1,0:T(8,128)(2,1)} async-done(((bf16[2,256,128]{2,1,0:T(8,128)(2,1)}), bf16[2,256,1024]{2,1,0:T(8,128)(2,1)}) %all-gather.5.cloned.1.call-update) | async-done | bytes 1048592 | tf_op jit(solution)/shard_map/all_gather | solution.py:13
  190.3 2.5 fusion.2
  192.9 2.0 copy.13
  194.9 3.4 %fusion.18 = f32[1024,1,2]{2,1,0:T(1,128)} fusion(bf16[2,256,1024]{1,0,2:T(2,128)(2,1)} %copy.13, bf16[1024,256,1]{1,0,2:T(8,128)(2,1)} %bitcast.49), kind=kOutput, calls=%fused_computation.19 | convolution fusion | flops 1048576 | bytes 1581056 | tf_op jit(solution)/shard_map/mv,kvm->km/dot_general | solution.py:20
  198.3 0.0 reduce-scatter.17.cloned.1.call-update
  198.3 0.0 reduce-scatter.23.cloned.1.call-start
  198.3 22.0 %reduce-scatter.17.cloned.1.call-done = f32[2,256]{0,1:T(8,128)} async-done(((f32[2,1024]{0,1:T(8,128)}), f32[2,256]{0,1:T(8,128)}) %reduce-scatter.17.cloned.1.call-update) | async-done | bytes 2064 | tf_op jit(solution)/shard_map/reduce_scatter | solution.py:21
  220.3 3.4 %convolution_convert_fusion = bf16[2,8192]{1,0:T(2,128)(2,1)S(1)} fusion(bf16[8192,256]{1,0:T(8,128)(2,1)} %param.9, f32[2,256]{0,1:T(8,128)} %reduce-scatter.17.cloned.1.call-done), kind=kOutput, calls=%fused_computation | convolution fusion | flops 8405504 | bytes 4229120 | tf_op jit(solution)/shard_map/km,nm->kn/dot_general | solution.py:22
  223.7 0.0 copy-start.3
  223.7 1.9 copy.19
  225.7 0.0 reduce-scatter.23.cloned.1.call-update
  225.7 0.0 reduce-scatter.25.cloned.1.call-start
  225.7 39.5 %reduce-scatter.23.cloned.1.call-done = bf16[1024,2]{1,0:T(8,128)(2,1)} async-done(((bf16[8192,2]{1,0:T(8,128)(2,1)}), bf16[1024,2]{1,0:T(8,128)(2,1)}) %reduce-scatter.23.cloned.1.call-update) | async-done | bytes 4112
  265.2 1.1 copy.20
  266.3 11.9 %psum.15 = f32[2,1024]{1,0:T(2,128)S(1)} all-reduce(bf16[2,1024]{1,0:T(2,128)(2,1)S(1)} %copy.20), channel_id=1, replica_groups=mesh['pts'=8,'val'=4] {'val'}, use_global_device_ids=true, to_apply=%region_6.0 | all-reduce | flops 2048 | bytes 12288 | tf_op jit(solution)/shard_map/psum | solution.py:26
  278.2 0.0 copy-done.3
  278.2 2.2 fusion.11
  280.4 2.5 copy.21
  283.0 0.0 copy-start.2
  283.0 1.2 copy.24
  284.2 0.0 reduce-scatter.25.cloned.1.call-update
  284.2 33.3 %reduce-scatter.25.cloned.1.call-done = bf16[128,512]{1,0:T(8,128)(2,1)} async-done(((bf16[1024,512]{1,0:T(8,128)(2,1)}), bf16[128,512]{1,0:T(8,128)(2,1)}) %reduce-scatter.25.cloned.1.call-update) | async-done | bytes 131088
  317.5 0.9 reshape.22
  318.5 0.1 copy.22
  318.6 0.0 copy-done.2
  318.6 0.8 convert_subtract_fusion
Async XLA Ops:
  7.2 28.9 %copy-start = (bf16[1024,1024]{1,0:T(8,128)(2,1)S(1)}, bf16[1024,1024]{1,0:T(8,128)(2,1)}, u32[]{:S(2)}) copy-start(bf16[1024,1024]{1,0:T(8,128)(2,1)} %param.8) | copy-start | bytes 6291460
  7.2 28.9 %all-gather.3.cloned.1.call-start = ((), (), s32[]{:S(2)}) async-start(), calls=%async_computation.6 | async-start | bytes 1179648 | tf_op jit(solution)/shard_map/all_gather | solution.py:13
  7.9 58.2 %reduce-scatter.15.cloned.1.call-start = ((), (), s32[]{:S(2)}) async-start(), calls=%async_computation.7 | async-start | bytes 655360 | tf_op jit(solution)/shard_map/reduce_scatter | solution.py:21
  44.1 66.9 %reduce-scatter.19.cloned.1.call-start = ((), (), s32[]{:S(2)}) async-start(), calls=%async_computation.10 | async-start | bytes 2359296
  71.4 93.1 %reduce-scatter.21.cloned.1.call-start = ((), (), s32[]{:S(2)}) async-start(), calls=%async_computation.11 | async-start | bytes 1179648
  129.9 2.1 copy-start.4
  129.9 35.7 %copy-start.1 = (bf16[2,256,128]{2,1,0:T(8,128)(2,1)S(1)}, bf16[2,256,128]{2,1,0:T(8,128)(2,1)}, u32[]{:S(2)}) copy-start(bf16[2,256,128]{2,1,0:T(8,128)(2,1)} %param.6) | copy-start | bytes 393220
  131.2 59.2 %all-gather.5.cloned.1.call-start = ((), (), s32[]{:S(2)}) async-start(), calls=%async_computation.8 | async-start | bytes 1179648 | tf_op jit(solution)/shard_map/all_gather | solution.py:13
  166.4 53.9 %reduce-scatter.17.cloned.1.call-start = ((), (), s32[]{:S(2)}) async-start(), calls=%async_computation.9 | async-start | bytes 655360 | tf_op jit(solution)/shard_map/reduce_scatter | solution.py:21
  198.3 66.9 %reduce-scatter.23.cloned.1.call-start = ((), (), s32[]{:S(2)}) async-start(), calls=%async_computation.12 | async-start | bytes 2359296
  223.7 54.5 %copy-start.3 = (f32[256,1024]{1,0:T(8,128)S(1)}, f32[256,1024]{1,0:T(8,128)}, u32[]{:S(2)}) copy-start(f32[256,1024]{1,0:T(8,128)} %copy.9) | copy-start | bytes 3145732
  225.7 91.9 %reduce-scatter.25.cloned.1.call-start = ((), (), s32[]{:S(2)}) async-start(), calls=%async_computation.13 | async-start | bytes 1179648
  283.0 35.7 %copy-start.2 = (bf16[2,256,128]{2,1,0:T(8,128)(2,1)S(1)}, bf16[2,256,128]{2,1,0:T(8,128)(2,1)}, u32[]{:S(2)}) copy-start(bf16[2,256,128]{2,1,0:T(8,128)(2,1)} %get-tuple-element.2) | copy-start | bytes 393220
Sparse Core Ops, SparseCore 0:
  9.9 26.1 all-gather.2
  44.2 21.8 reduce-scatter.14
  71.6 39.3 reduce-scatter.18
  131.3 33.1 reduce-scatter.20
  166.8 23.4 all-gather.4
  198.4 21.8 reduce-scatter.16
  225.8 39.3 reduce-scatter.22
  284.3 33.1 reduce-scatter.24
where the time goes:
time: 327 us; the launch traced here: 326 us
  waiting for transfers between devices  239 us (73%)
  matrix products  24.3 us (7%)
  blocking collectives  23.8 us (7%)
  local copies, waits for them, and re-layouts  21.7 us (7%)
  between operations  14.3 us (4%)
    unnamed x12, waiting for transfers between devices  143 us
    all_gather x2, waiting for transfers between devices, gathered_inner(): lax.all_gather(local_trial, 'pts', axis=2, tiled=True)  52 us
    reduce_scatter x2, waiting for transfers between devices, orbital_terms(): lax.psum_scatter(rho_part, 'val', scatter_dimension=1, tiled=True)  43.9 us
    psum x2, blocking collectives, orbital_terms(): image = lax.psum(image_rows, 'val')  23.8 us
    unnamed x22, local copies, waits for them, and re-layouts  15.6 us
    dot_general x2, matrix products, orbital_terms(): jnp.einsum('km,nm->kn', rho, kernel, preferred_element_type=jnp.float32)  6.88 us
    dot_general x2, matrix products, orbital_terms(): rho_part = jnp.einsum('mv,kvm->km', psi_val.astype(jnp.float32), inner)  6.78 us
  transfers between devices with their start and end apart: 8, of which 8 were waited for; matrix products, arithmetic and copies ran while one was open for 1% of the time, Pallas kernels for 0%

commit v1 on v0

--- a/solution.py
+++ b/solution.py
@@ -7,10 +7,15 @@
 half_width = 1.25
 
 
+def gather_from_all(x, axis, dim):
+    copies = jnp.concatenate([x] * lax.axis_size(axis), axis=dim)
+    return lax.all_to_all(copies, axis, dim, dim, tiled=True)
+
+
 def gathered_inner(local_trial, psi_cond):
     return jnp.einsum(
         "kvc,mc->kvm",
-        lax.all_gather(local_trial, "pts", axis=2, tiled=True),
+        gather_from_all(local_trial, "pts", 2),
         psi_cond,
         preferred_element_type=jnp.float32,
     )

time: 327 us -> 333 us (1.018)
  waiting for transfers between devices: 239 us -> 185 us
  blocking collectives: 23.8 us -> 62.1 us
  local copies, waits for them, and re-layouts: 21.7 us -> 45.1 us
    all_gather x2 -> x0, waiting for transfers between devices: 52 us -> none  [gathered_inner(): lax.all_gather(local_trial, 'pts', axis=2, tiled=True)]
    all_to_all x0 -> x2, blocking collectives: none -> 38.2 us  [gather_from_all(): return lax.all_to_all(copies, axis, dim, dim, tiled=True)]
    unnamed x22 -> x33, local copies, waits for them, and re-layouts: 15.6 us -> 31.7 us
    concatenate x0 -> x4, local copies, waits for them, and re-layouts: none -> 7.26 us  [gather_from_all(): copies = jnp.concatenate([x] * lax.axis_size(axis), axis=dim)]
    unnamed x12 -> x10, waiting for transfers between devices: 143 us -> 142 us
  transfers between devices with their start and end apart: 8 -> 6, of which waited for: 8 -> 6; matrix products, arithmetic and copies ran while one was open for 1% -> 1% of each run, Pallas kernels for 0% -> 0%
where the time goes in v1:
time: 333 us; the launch traced here: 332 us
  waiting for transfers between devices  185 us (56%)
  blocking collectives  62.1 us (19%)
  local copies, waits for them, and re-layouts  45.1 us (14%)
  matrix products  22.7 us (7%)
  between operations  14.3 us (4%)
    unnamed x10, waiting for transfers between devices  142 us
    reduce_scatter x2, waiting for transfers between devices, orbital_terms(): lax.psum_scatter(rho_part, 'val', scatter_dimension=1, tiled=True)  42.3 us
    all_to_all x2, blocking collectives, gather_from_all(): return lax.all_to_all(copies, axis, dim, dim, tiled=True)  38.2 us
    unnamed x33, local copies, waits for them, and re-layouts  31.7 us
    psum x2, blocking collectives, orbital_terms(): image = lax.psum(image_rows, 'val')  23.9 us
    dot_general x2, matrix products, orbital_terms(): jnp.einsum('km,nm->kn', rho, kernel, preferred_element_type=jnp.float32)  7.52 us
    concatenate x4, local copies, waits for them, and re-layouts, gather_from_all(): copies = jnp.concatenate([x] * lax.axis_size(axis), axis=dim)  7.26 us
    dot_general x2, matrix products, orbital_terms(): rho_part = jnp.einsum('mv,kvm->km', psi_val.astype(jnp.float32), inner)  6.81 us
  transfers between devices with their start and end apart: 6, of which 6 were waited for; matrix products, arithmetic and copies ran while one was open for 1% of the time, Pallas kernels for 0%

profile of v1, /device:TPU:0, one launch (start us, length us, event | category | flops | bytes accessed | tf_op | source)
XLA Modules:
  0.0 331.8 jit_solution(13152471250227471124)
XLA Ops:
  7.2 0.0 reduce-scatter.15.cloned.1.call-start
  7.2 1.7 constant_dynamic-update-slice_fusion.7
  8.9 1.6 constant_dynamic-update-slice_fusion.6
  10.5 1.6 constant_dynamic-update-slice_fusion.5
  12.1 1.6 constant_dynamic-update-slice_fusion.4
  13.7 1.6 constant_dynamic-update-slice_fusion.3
  15.3 1.6 constant_dynamic-update-slice_fusion.2
  16.9 1.6 constant_dynamic-update-slice_fusion.1
  18.5 1.6 constant_dynamic-update-slice_fusion
  20.1 2.5 copy.20
  22.6 20.3 %all_to_all.10 = bf16[2,256,1024]{1,0,2:T(2,128)(2,1)S(1)} all-to-all(bf16[2,256,1024]{1,0,2:T(2,128)(2,1)S(1)} %copy.20), channel_id=1, replica_groups=mesh['pts'=8,'val'=4] {'pts'}, dimensions={2} | all-to-all | bytes 2097152 | tf_op jit(solution)/shard_map/all_to_all | solution.py:12
  42.9 1.3 fusion.6
  44.2 2.0 copy.24
  46.3 3.4 %fusion.22 = f32[1024,1,2]{2,1,0:T(1,128)} fusion(bf16[2,256,1024]{1,0,2:T(2,128)(2,1)} %copy.24, bf16[1024,256,1]{1,0,2:T(8,128)(2,1)} %bitcast.46), kind=kOutput, calls=%fused_computation.23 | convolution fusion | flops 1048576 | bytes 1581056 | tf_op jit(solution)/shard_map/mv,kvm->km/dot_general | solution.py:25
  49.7 0.0 reduce-scatter.19.cloned.1.call-start
  49.7 21.3 %reduce-scatter.15.cloned.1.call-done = f32[2,256]{0,1:T(8,128)} async-done(((f32[2,1024]{0,1:T(8,128)}), f32[2,256]{0,1:T(8,128)}) %reduce-scatter.15.cloned.1.call-update) | async-done | bytes 2064 | tf_op jit(solution)/shard_map/reduce_scatter | solution.py:26
  71.1 3.4 %convolution_convert_fusion.1 = bf16[2,8192]{1,0:T(2,128)(2,1)S(1)} fusion(bf16[8192,256]{1,0:T(8,128)(2,1)} %param.9, f32[2,256]{0,1:T(8,128)} %reduce-scatter.15.cloned.1.call-done), kind=kOutput, calls=%fused_computation.1 | convolution fusion | flops 8405504 | bytes 4229120 | tf_op jit(solution)/shard_map/km,nm->kn/dot_general | solution.py:27
  74.5 1.9 copy.29
  76.4 0.0 reduce-scatter.19.cloned.1.call-update
  76.4 0.0 reduce-scatter.21.cloned.1.call-start
  76.5 1.1 convert_bitcast_fusion
  77.6 1.3 copy.19
  78.9 37.0 %reduce-scatter.19.cloned.1.call-done = bf16[1024,2]{1,0:T(8,128)(2,1)} async-done(((bf16[8192,2]{1,0:T(8,128)(2,1)}), bf16[1024,2]{1,0:T(8,128)(2,1)}) %reduce-scatter.19.cloned.1.call-update) | async-done | bytes 4112
  115.9 1.1 copy.30
  117.0 11.9 %psum.14 = f32[2,1024]{1,0:T(2,128)S(1)} all-reduce(bf16[2,1024]{1,0:T(2,128)(2,1)S(1)} %copy.30), channel_id=1, replica_groups=mesh['pts'=8,'val'=4] {'val'}, use_global_device_ids=true, to_apply=%region_2.0 | all-reduce | flops 2048 | bytes 12288 | tf_op jit(solution)/shard_map/psum | solution.py:31
  128.9 3.5 %fusion.8 = bf16[2,256,1024]{2,1,0:T(8,128)(2,1)} fusion(bf16[1024,1024]{1,0:T(8,128)(2,1)S(1)} %copy-done, f32[2,1024]{1,0:T(2,128)S(1)} %psum.14, f32[256,1024]{1,0:T(8,128)} %copy.19), kind=kOutput, calls=%fused_computation.12 | convolution fusion | flops 1075314688 | bytes 4202496 | tf_op jit(solution)/shard_map/kvm,mc->kvc/dot_general | solution.py:35
  132.4 2.5 copy.31
  134.9 1.2 copy.37
  136.1 0.0 reduce-scatter.21.cloned.1.call-update
  136.1 0.0 reduce-scatter.17.cloned.1.call-start
  136.2 0.8 dynamic-slice.4
  137.0 0.1 subtract_add_fusion
  137.1 32.4 %reduce-scatter.21.cloned.1.call-done = bf16[128,512]{1,0:T(8,128)(2,1)} async-done(((bf16[1024,512]{1,0:T(8,128)(2,1)}), bf16[128,512]{1,0:T(8,128)(2,1)}) %reduce-scatter.21.cloned.1.call-update) | async-done | bytes 131088
  169.5 0.9 reshape.18
  170.4 0.1 copy.32
  170.6 0.8 constant_dynamic-update-slice_fusion.15
  171.4 0.7 constant_dynamic-update-slice_fusion.14
  172.1 0.7 constant_dynamic-update-slice_fusion.13
  172.8 0.7 constant_dynamic-update-slice_fusion.12
  173.5 0.7 constant_dynamic-update-slice_fusion.11
  174.1 0.7 constant_dynamic-update-slice_fusion.10
  174.8 0.7 constant_dynamic-update-slice_fusion.9
  175.5 0.7 constant_dynamic-update-slice_fusion.8
  176.2 2.5 copy.22
  178.7 17.9 %all_to_all.11 = bf16[2,256,1024]{1,0,2:T(2,128)(2,1)S(1)} all-to-all(bf16[2,256,1024]{1,0,2:T(2,128)(2,1)S(1)} %copy.22), channel_id=1, replica_groups=mesh['pts'=8,'val'=4] {'pts'}, dimensions={2} | all-to-all | bytes 2097152 | tf_op jit(solution)/shard_map/all_to_all | solution.py:12
  196.6 1.3 fusion.2
  197.9 2.0 copy.27
  200.0 3.4 %fusion.20 = f32[1024,1,2]{2,1,0:T(1,128)} fusion(bf16[2,256,1024]{1,0,2:T(2,128)(2,1)} %copy.27, bf16[1024,256,1]{1,0,2:T(8,128)(2,1)} %bitcast.47), kind=kOutput, calls=%fused_computation.21 | convolution fusion | flops 1048576 | bytes 1581056 | tf_op jit(solution)/shard_map/mv,kvm->km/dot_general | solution.py:25
  203.4 0.0 reduce-scatter.17.cloned.1.call-update
  203.4 0.0 reduce-scatter.23.cloned.1.call-start
  203.4 21.0 %reduce-scatter.17.cloned.1.call-done = f32[2,256]{0,1:T(8,128)} async-done(((f32[2,1024]{0,1:T(8,128)}), f32[2,256]{0,1:T(8,128)}) %reduce-scatter.17.cloned.1.call-update) | async-done | bytes 2064 | tf_op jit(solution)/shard_map/reduce_scatter | solution.py:26
  224.5 4.1 %convolution_convert_fusion = bf16[2,8192]{1,0:T(2,128)(2,1)} fusion(bf16[8192,256]{1,0:T(8,128)(2,1)} %param.9, f32[2,256]{0,1:T(8,128)} %reduce-scatter.17.cloned.1.call-done), kind=kOutput, calls=%fused_computation | convolution fusion | flops 8405504 | bytes 4229120 | tf_op jit(solution)/shard_map/km,nm->kn/dot_general | solution.py:27
  228.6 2.7 copy.33
  231.3 0.0 reduce-scatter.25.cloned.1.call-start
  231.3 39.4 %reduce-scatter.23.cloned.1.call-done = bf16[1024,2]{1,0:T(8,128)(2,1)} async-done(((bf16[8192,2]{1,0:T(8,128)(2,1)}), bf16[1024,2]{1,0:T(8,128)(2,1)}) %reduce-scatter.23.cloned.1.call-update) | async-done | bytes 4112
  270.7 1.1 copy.34
  271.8 11.9 %psum.15 = f32[2,1024]{1,0:T(2,128)S(1)} all-reduce(bf16[2,1024]{1,0:T(2,128)(2,1)S(1)} %copy.34), channel_id=1, replica_groups=mesh['pts'=8,'val'=4] {'val'}, use_global_device_ids=true, to_apply=%region_6.0 | all-reduce | flops 2048 | bytes 12288 | tf_op jit(solution)/shard_map/psum | solution.py:31
  283.7 2.2 fusion.11
  286.0 2.5 copy.35
  288.5 1.2 copy.38
  289.7 33.3 %reduce-scatter.25.cloned.1.call-done = bf16[128,512]{1,0:T(8,128)(2,1)} async-done(((bf16[1024,512]{1,0:T(8,128)(2,1)}), bf16[128,512]{1,0:T(8,128)(2,1)}) %reduce-scatter.25.cloned.1.call-update) | async-done | bytes 131088
  323.1 0.9 reshape.22
  324.0 0.1 copy.36
  324.2 0.8 convert_subtract_fusion
  (11 shorter events, 0.1 us)
Async XLA Ops:
  7.2 35.7 %copy-start = (bf16[1024,1024]{1,0:T(8,128)(2,1)S(1)}, bf16[1024,1024]{1,0:T(8,128)(2,1)}, u32[]{:S(2)}) copy-start(bf16[1024,1024]{1,0:T(8,128)(2,1)} %param.8) | copy-start | bytes 6291460
  7.2 63.9 %reduce-scatter.15.cloned.1.call-start = ((), (), s32[]{:S(2)}) async-start(), calls=%async_computation.8 | async-start | bytes 655360 | tf_op jit(solution)/shard_map/reduce_scatter | solution.py:26
  49.7 66.2 %reduce-scatter.19.cloned.1.call-start = ((), (), s32[]{:S(2)}) async-start(), calls=%async_computation.10 | async-start | bytes 2359296
  76.4 93.1 %reduce-scatter.21.cloned.1.call-start = ((), (), s32[]{:S(2)}) async-start(), calls=%async_computation.11 | async-start | bytes 1179648
  134.9 2.1 copy-start.3
  134.9 35.7 %copy-start.1 = (bf16[2,256,128]{2,1,0:T(8,128)(2,1)S(1)}, bf16[2,256,128]{2,1,0:T(8,128)(2,1)}, u32[]{:S(2)}) copy-start(bf16[2,256,128]{2,1,0:T(8,128)(2,1)} %param.6) | copy-start | bytes 393220
  136.1 88.3 %reduce-scatter.17.cloned.1.call-start = ((), (), s32[]{:S(2)}) async-start(), calls=%async_computation.9 | async-start | bytes 655360 | tf_op jit(solution)/shard_map/reduce_scatter | solution.py:26
  203.4 67.3 %reduce-scatter.23.cloned.1.call-start = ((), (), s32[]{:S(2)}) async-start(), calls=%async_computation.12 | async-start | bytes 2359296
  228.6 55.2 %copy-start.2 = (f32[256,1024]{1,0:T(8,128)S(1)}, f32[256,1024]{1,0:T(8,128)}, u32[]{:S(2)}) copy-start(f32[256,1024]{1,0:T(8,128)} %copy.19) | copy-start | bytes 3145732
  231.3 91.8 %reduce-scatter.25.cloned.1.call-start = ((), (), s32[]{:S(2)}) async-start(), calls=%async_computation.13 | async-start | bytes 1179648
Sparse Core Ops, SparseCore 0:
  49.8 21.1 reduce-scatter.14
  76.6 39.2 reduce-scatter.18
  136.3 33.1 reduce-scatter.20
  203.5 20.9 reduce-scatter.16
  231.4 39.2 reduce-scatter.22
  289.9 33.1 reduce-scatter.24
